TPU v7x, 32 devices: a whole 2x2x4 slice. The times are simulated.
32 devices in a mesh: seq: 8 (over z, y), tp: 4 (over x, core).
Axes of the slice: x: 2, y: 2, z: 4, core: 2. Of those that a mesh axis runs over, the one named last changes fastest.
Arguments:
- prefill_tokens: bfloat16 [4096, 2304], P('seq'), may hold values from -6 to 6
- decode_tokens: bfloat16 [64, 2304], P('seq'), may hold values from -6 to 6
- attention_gain: float32 [2304], replicated, may hold values from 0.5 to 1.5
- qkv_weight: bfloat16 [2304, 3, 2304], P(None, None, 'tp'), may hold values from -0.125 to 0.125
- out_weight: bfloat16 [2304, 2304], P('tp'), may hold values from -0.375 to 0.375
- feedforward_gain: float32 [2304], replicated, may hold values from 0.5 to 1.5
- prefill_cache: bfloat16 [8, 2, 1024, 2304], P('seq', None, None, 'tp'), may hold values from -420 to 420
- prefill_offsets: int32 [8], P('seq'), may hold values from 0 to 1024, as said below
- decode_cache: bfloat16 [64, 2, 256, 2304], P('seq', None, None, 'tp'), may hold values from -420 to 420
- decode_lengths: int32 [64], P('seq'), may hold values from 1 to 256, as said below
- request_slot: int32 [64], replicated, may hold values from 0 to 63, each once
Outputs:
- prefill_hidden: bfloat16 [4096, 2304], P('seq')
- decode_hidden: bfloat16 [64, 2304], P('seq')
- prefill_normed: bfloat16 [4096, 2304], P('seq')
- decode_normed: bfloat16 [64, 2304], P('seq')
Inputs may be any that keep to these rules, and one draw needn't show every extreme that they name: `request_slot`: each slot is named by exactly one request. `decode_lengths`: some slot holds exactly 256 positions. `prefill_offsets`: some request has exactly 1024 cached positions.
All inputs are finite; a program needn't handle non-finite values.
Results may differ from a plain program's by a relative error of at most 0.014.
The roundings to bfloat16 on the way count: a program that leaves them out, or rounds other values in their place, can miss the bound.
Values may be sent and summed in bfloat16 or wider, within the bound.
A program may use at most 128 MiB of HBM per device.

v0:
```python
import math
import jax
import jax.numpy as jnp
from jax import lax
from jax.sharding import PartitionSpec as P

HEAD = 64
RMS_EPSILON = 1e-05
ROPE_BASE = 10000.0
NEGATIVE = -1e30


def rms_norm(stream, gain):
    widened = stream.astype(jnp.float32)
    inverse = lax.rsqrt(jnp.mean(widened * widened, axis=-1, keepdims=True) + RMS_EPSILON)
    return widened * inverse * gain


def rotate(vectors, positions):
    half_dim = vectors.shape[-1] // 2
    exponent = jnp.arange(half_dim, dtype=jnp.float32) * (2.0 / vectors.shape[-1])
    frequency = ROPE_BASE ** (-exponent)
    angles = positions[:, None] * frequency[None, :]
    cosine = jnp.cos(angles)[:, None, :]
    sine_part = jnp.sin(angles)[:, None, :]
    first_half = vectors[..., :half_dim]
    second_half = vectors[..., half_dim:]
    return jnp.concatenate(
        [
            first_half * cosine - second_half * sine_part,
            second_half * cosine + first_half * sine_part,
        ],
        axis=-1,
    )


def prefill_attention(block_rows, cache_pair, offset, head_count):
    span_rows = block_rows.shape[0]
    cache_len = cache_pair.shape[1]
    score_scale = 1.0 / math.sqrt(HEAD)
    positions = offset.astype(jnp.float32) + jnp.arange(span_rows, dtype=jnp.float32)
    queries = rotate(
        block_rows[:, 0].reshape(span_rows, head_count, HEAD).astype(jnp.float32), positions
    ).astype(jnp.bfloat16)
    new_keys = rotate(
        block_rows[:, 1].reshape(span_rows, head_count, HEAD).astype(jnp.float32), positions
    ).astype(jnp.bfloat16)
    new_values = block_rows[:, 2].reshape(span_rows, head_count, HEAD)
    cache_keys = cache_pair[0].reshape(cache_len, head_count, HEAD)
    cache_values = cache_pair[1].reshape(cache_len, head_count, HEAD)
    cache_scores = (
        jnp.einsum("qhe,khe->hqk", queries, cache_keys, preferred_element_type=jnp.float32)
        * score_scale
    )
    span_scores = (
        jnp.einsum("qhe,khe->hqk", queries, new_keys, preferred_element_type=jnp.float32)
        * score_scale
    )
    cache_visible = (jnp.arange(cache_len, dtype=jnp.int32) < offset)[None, None, :]
    causal = (
        jnp.arange(span_rows, dtype=jnp.int32)[None, :]
        <= jnp.arange(span_rows, dtype=jnp.int32)[:, None]
    )[None]
    cache_scores = jnp.where(cache_visible, cache_scores, NEGATIVE)
    span_scores = jnp.where(causal, span_scores, NEGATIVE)
    row_peak = jnp.maximum(
        jnp.max(cache_scores, axis=-1, keepdims=True), jnp.max(span_scores, axis=-1, keepdims=True)
    )
    cache_exp = jnp.exp(cache_scores - row_peak)
    span_exp = jnp.exp(span_scores - row_peak)
    denominator = jnp.sum(cache_exp, axis=-1, keepdims=True) + jnp.sum(
        span_exp, axis=-1, keepdims=True
    )
    cache_weights = (cache_exp / denominator).astype(jnp.bfloat16)
    span_weights = (span_exp / denominator).astype(jnp.bfloat16)
    attended = jnp.einsum(
        "hqk,khe->qhe", cache_weights, cache_values, preferred_element_type=jnp.float32
    )
    attended = attended + jnp.einsum(
        "hqk,khe->qhe", span_weights, new_values, preferred_element_type=jnp.float32
    )
    return attended.reshape(span_rows, head_count * HEAD).astype(jnp.bfloat16)


def decode_attention(routed, cache_block, lengths, head_count):
    slot_count = routed.shape[0]
    cache_len = cache_block.shape[2]
    score_scale = 1.0 / math.sqrt(HEAD)
    positions = lengths.astype(jnp.float32)
    queries = rotate(
        routed[:, 0].reshape(slot_count, head_count, HEAD).astype(jnp.float32), positions
    ).astype(jnp.bfloat16)
    new_keys = rotate(
        routed[:, 1].reshape(slot_count, head_count, HEAD).astype(jnp.float32), positions
    ).astype(jnp.bfloat16)
    new_values = routed[:, 2].reshape(slot_count, head_count, HEAD)
    cache_keys = cache_block[:, 0].reshape(slot_count, cache_len, head_count, HEAD)
    cache_values = cache_block[:, 1].reshape(slot_count, cache_len, head_count, HEAD)
    cache_scores = (
        jnp.einsum("she,skhe->shk", queries, cache_keys, preferred_element_type=jnp.float32)
        * score_scale
    )
    self_scores = (
        jnp.einsum("she,she->sh", queries, new_keys, preferred_element_type=jnp.float32)
        * score_scale
    )
    visible = (jnp.arange(cache_len, dtype=jnp.int32)[None, :] < lengths[:, None])[:, None, :]
    cache_scores = jnp.where(visible, cache_scores, NEGATIVE)
    row_peak = jnp.maximum(jnp.max(cache_scores, axis=-1), self_scores)
    cache_exp = jnp.exp(cache_scores - row_peak[..., None])
    self_exp = jnp.exp(self_scores - row_peak)
    denominator = jnp.sum(cache_exp, axis=-1) + self_exp
    cache_weights = (cache_exp / denominator[..., None]).astype(jnp.bfloat16)
    self_weights = (self_exp / denominator).astype(jnp.bfloat16)
    attended = jnp.einsum(
        "shk,skhe->she", cache_weights, cache_values, preferred_element_type=jnp.float32
    )
    attended = attended + self_weights.astype(jnp.float32)[..., None] * new_values.astype(
        jnp.float32
    )
    return attended.reshape(slot_count, head_count * HEAD).astype(jnp.bfloat16)


def local(
    prefill_tokens,
    decode_tokens,
    attention_gain,
    qkv_weight,
    out_weight,
    feedforward_gain,
    prefill_cache,
    prefill_offsets,
    decode_cache,
    decode_lengths,
    request_slot,
):
    span_rows = prefill_tokens.shape[0]
    decode_rows = decode_tokens.shape[0]
    model_width = prefill_tokens.shape[1]
    local_width = out_weight.shape[0]
    head_count = local_width // HEAD
    tokens_all = jnp.concatenate([prefill_tokens, decode_tokens], axis=0)
    normed_in = rms_norm(tokens_all, attention_gain).astype(jnp.bfloat16)
    projected = jnp.dot(
        normed_in,
        qkv_weight.reshape(model_width, 3 * local_width),
        preferred_element_type=jnp.float32,
    ).astype(jnp.bfloat16)
    projected = projected.reshape(-1, 3, local_width)
    prefill_block = projected[:span_rows]
    decode_block = projected[span_rows:]
    seq_rank = lax.axis_index("seq")
    own_slots = seq_rank * decode_rows + jnp.arange(decode_rows, dtype=jnp.int32)
    arrived = lax.all_gather(decode_block, "seq", axis=0, tiled=True)
    picker = (request_slot[None, :] == own_slots[:, None]).astype(jnp.bfloat16)
    routed = jnp.einsum("sr,rcw->scw", picker, arrived, preferred_element_type=jnp.float32).astype(
        jnp.bfloat16
    )
    slot_results = decode_attention(routed, decode_cache, decode_lengths, head_count)
    prefill_attended = prefill_attention(
        prefill_block, prefill_cache[0], prefill_offsets[0], head_count
    )
    my_slots = lax.dynamic_slice_in_dim(request_slot, seq_rank * decode_rows, decode_rows)
    shard_piece = lax.all_gather(slot_results, "seq", axis=0, tiled=True)
    slot_ids = jnp.arange(shard_piece.shape[0], dtype=jnp.int32)
    picker = (my_slots[:, None] == slot_ids[None, :]).astype(jnp.bfloat16)
    returned = jnp.dot(picker, shard_piece, preferred_element_type=jnp.float32).astype(jnp.bfloat16)
    attended_all = jnp.concatenate([prefill_attended, returned], axis=0)
    partial_value = jnp.dot(attended_all, out_weight, preferred_element_type=jnp.float32)
    combined = lax.psum(partial_value.astype(jnp.bfloat16), "tp").astype(jnp.float32)
    hidden = (tokens_all.astype(jnp.float32) + combined).astype(jnp.bfloat16)
    normed = rms_norm(hidden, feedforward_gain).astype(jnp.bfloat16)
    return (hidden[:span_rows], hidden[span_rows:], normed[:span_rows], normed[span_rows:])


def solution(mesh):
    placed = (
        P("seq", None),
        P("seq", None),
        P(),
        P(None, None, "tp"),
        P("tp", None),
        P(),
        P("seq", None, None, "tp"),
        P("seq"),
        P("seq", None, None, "tp"),
        P("seq"),
        P(),
    )
    return jax.shard_map(
        local,
        mesh=mesh,
        in_specs=placed,
        out_specs=(P("seq", None), P("seq", None), P("seq", None), P("seq", None)),
        check_vma=False,
    )
```

profile of v0, /device:TPU:0, one launch (start us, length us, event | category | flops | bytes accessed | tf_op | source)
XLA Modules:
  0.0 215.5 jit_solution(18062923695454391334)
XLA Ops:
  7.2 0.8 convert_element_type.115
  8.1 0.7 iota_compare_fusion.1
  8.8 2.4 %fusion.8 = f32[520]{0:T(1024)S(1)} fusion(bf16[8,2304]{1,0:T(8,128)(2,1)} %param.12, bf16[512,2304]{1,0:T(8,128)(2,1)} %param.11), kind=kLoop, calls=%fused_computation.19 | loop fusion | flops 7187960 | bytes 2398240 | tf_op jit(solution)/shard_map/reduce_sum | solution.py:15
  11.2 8.6 %convolution_convert_fusion.1 = bf16[520,1728]{1,0:T(8,128)(2,1)S(1)} fusion(bf16[2304,1728]{0,1:T(8,128)(2,1)} %bitcast.71, f32[2304]{0:T(1024)} %param.13, f32[520]{0:T(1024)S(1)} %add_rsqrt_fusion.1, bf16[8,2304]{1,0:T(8,128)(2,1)} %param.12, bf16[512,2304]{1,0:T(8,128)(2,1)} %param.11), kind=kOutput, calls=%fused_computation.25 | convolution fusion | flops 4149849600 | bytes 12167200 | tf_op jit(solution)/shard_map/dot_general | solution.py:144
  19.8 1.4 slice.106
  21.2 0.1 iota_compare_fusion
  21.3 2.5 %fusion.55 = (bf16[8,1,256,576]{2,3,1,0:T(8,128)(2,1)}, bf16[8,1,256,576]{2,3,1,0:T(8,128)(2,1)}) fusion(bf16[8,2,256,576]{2,3,1,0:T(8,128)(2,1)S(1)} %bitcast.64), kind=kLoop, calls=%fused_computation.103 | loop fusion | bytes 9437184 | tf_op jit(solution)/shard_map/slice | solution.py:97
  23.8 0.1 slice.92
  23.9 32.5 %all_gather.6 = bf16[64,3,576]{2,0,1:T(8,128)(2,1)S(1)} all-gather(bf16[8,3,576]{2,0,1:T(8,128)(2,1)S(1)} %copy.25), channel_id=1, replica_groups=mesh['seq'=8,'tp'=4] {'seq'}, dimensions={0}, use_global_device_ids=true | all-gather | bytes 248832 | tf_op jit(solution)/shard_map/all_gather | solution.py:154
  56.5 0.2 convolution_convert_fusion.2
  56.7 0.1 reshape.210
  56.8 0.1 multiply_cosine_fusion.1
  56.9 0.1 subtract_convert_fusion.2
  57.1 0.1 fusion.38
  57.2 0.2 fusion.32
  57.3 0.1 copy.34
  57.4 2.1 fusion.35
  59.5 0.1 fusion.34
  59.6 0.2 fusion.33
  59.8 0.1 fusion.37
  59.9 0.1 reshape.211
  60.1 2.4 %fusion.29 = f32[8,9,1,64]{3,2,1,0:T(1,128)S(1)} fusion(bf16[8,256,9,64]{1,3,2,0:T(8,128)(2,1)} %bitcast.68, bf16[8,9,256,1]{2,0,1,3:T(8,128)(2,1)S(1)} %fusion.37), kind=kOutput, calls=%fused_computation.53 | convolution fusion | flops 2359296 | bytes 2414592 | tf_op jit(solution)/shard_map/shk,skhe->she/dot_general | solution.py:115
  62.4 0.1 fusion.31
  62.5 0.1 convert_element_type.124
  62.6 30.5 %all_gather.7 = bf16[64,576]{1,0:T(8,128)(2,1)S(1)} all-gather(bf16[8,576]{1,0:T(8,128)(2,1)S(1)} %convert_element_type.124), channel_id=1, replica_groups=mesh['seq'=8,'tp'=4] {'seq'}, dimensions={0}, use_global_device_ids=true | all-gather | bytes 82944 | tf_op jit(solution)/shard_map/all_gather | solution.py:164
  93.2 0.2 convolution_convert_fusion.3
  93.4 0.8 copy.27
  94.2 3.2 %fusion.56 = (bf16[1,1,1024,576]{2,3,1,0:T(8,128)(2,1)}, bf16[1,1,1024,576]{2,3,1,0:T(8,128)(2,1)}) fusion(bf16[1,2,1024,576]{2,3,1,0:T(8,128)(2,1)} %param.17), kind=kLoop, calls=%fused_computation.104 | loop fusion | bytes 4718592 | tf_op jit(solution)/shard_map/slice | solution.py:49
  98.1 4.0 %copy.23 = bf16[512,1728]{0,1:T(8,128)(2,1)} copy(bf16[512,1728]{1,0:T(8,128)(2,1)} %slice.106) | data formatting | bytes 3538944 | tf_op jit(solution)/shard_map/slice | solution.py:150
  102.1 2.4 %fusion.57 = (bf16[512,1,576]{0,2,1:T(8,128)(2,1)}, bf16[512,1,576]{0,2,1:T(8,128)(2,1)S(1)}, bf16[512,1,576]{0,2,1:T(8,128)(2,1)S(1)}) fusion(bf16[512,3,576]{0,2,1:T(8,128)(2,1)} %bitcast.62), kind=kLoop, calls=%fused_computation.105 | loop fusion | bytes 3538944 | tf_op jit(solution)/shard_map/slice | solution.py:48
  104.5 1.2 convert.40
  105.6 0.3 multiply_cosine_fusion
  105.9 0.1 convert.39
  106.1 1.6 subtract_convert_fusion
  107.7 2.8 %fusion = (f32[9,512]{1,0:T(8,128)S(1)}, f32[9,512,1024]{2,1,0:T(8,128)S(1)}) fusion(pred[1024]{0:T(1024)(128)(4,1)S(1)} %iota_compare_fusion.3, bf16[1024,9,64]{0,2,1:T(8,128)(2,1)S(1)} %bitcast.65, bf16[512,9,32]{0,2,1:T(8,128)(2,1)S(1)} %get-tuple-element.17, bf16[512,9,32]{0,2,1:T(8,128)(2,1)S(1)} %get-tuple-element.18), kind=kOutput, calls=%fused_computation.3 | convolution fusion | flops 619310592 | bytes 20663296 | tf_op jit(solution)/shard_map/qhe,khe->hqk/dot_general | solution.py:52
  110.5 5.3 %fusion.3 = (f32[9,512]{1,0:T(8,128)S(1)}, f32[9,512,512]{1,2,0:T(8,128)}) fusion(pred[512,512]{0,1:T(8,128)(4,1)S(1)} %iota_compare_fusion, bf16[512,9,32]{0,2,1:T(8,128)(2,1)S(1)} %get-tuple-element.14, bf16[512,9,32]{0,2,1:T(8,128)(2,1)S(1)} %get-tuple-element.13, bf16[512,9,32]{0,2,1:T(8,128)(2,1)S(1)} %get-tuple-element.17, ...), kind=kOutput, calls=%fused_computation.9 | convolution fusion | flops 311422464 | bytes 10897408 | tf_op jit(solution)/shard_map/qhe,khe->hqk/dot_general | solution.py:56
  115.8 4.5 %fusion.1 = f32[9,512]{1,0:T(8,128)S(1)} fusion(f32[9,512,1024]{2,1,0:T(8,128)S(1)} %get-tuple-element.35, f32[9,512]{1,0:T(8,128)S(1)} %max.11, pred[1024]{0:T(1024)(128)(4,1)S(1)} %iota_compare_fusion.3), kind=kLoop, calls=%fused_computation.4 | loop fusion | flops 18869760 | bytes 18912256 | tf_op jit(solution)/shard_map/reduce_sum | solution.py:71
  120.4 5.6 %fusion.4 = f32[9,512]{1,0:T(8,128)S(1)} fusion(f32[9,512,512]{1,2,0:T(8,128)} %get-tuple-element.37, f32[9,512]{1,0:T(8,128)S(1)} %max.11, pred[512,512]{0,1:T(8,128)(4,1)S(1)} %iota_compare_fusion), kind=kLoop, calls=%fused_computation.10 | loop fusion | flops 9432576 | bytes 9736192 | tf_op jit(solution)/shard_map/reduce_sum | solution.py:71
  126.0 7.1 %fusion.16 = f32[512,9,64]{0,2,1:T(8,128)} fusion(bf16[1024,9,64]{0,2,1:T(8,128)(2,1)} %bitcast.69, f32[9,512,1024]{2,1,0:T(8,128)S(1)} %get-tuple-element.35, f32[9,512]{1,0:T(8,128)S(1)} %add.78, f32[9,512]{1,0:T(8,128)S(1)} %max.11, pred[1024]{0:T(1024)(128)(4,1)S(1)} %iota_compare_fusion.3), kind=kOutput, calls=%fused_computation.29 | convolution fusion | flops 627572736 | bytes 21271552 | tf_op jit(solution)/shard_map/hqk,khe->qhe/dot_general | solution.py:76
  133.1 6.0 %fusion.19 = bf16[512,9,64]{0,2,1:T(8,128)(2,1)S(1)} fusion(f32[512,9,64]{0,2,1:T(8,128)} %fusion.16, bf16[512,9,64]{0,2,1:T(8,128)(2,1)S(1)} %bitcast.70, f32[9,512,512]{1,2,0:T(8,128)} %get-tuple-element.37, f32[9,512]{1,0:T(8,128)S(1)} %add.78, f32[9,512]{1,0:T(8,128)S(1)} %max.11, pred[512,512]{0,1:T(8,128)(4,1)S(1)} %iota_compare_fusion), kind=kOutput, calls=%fused_computation.32 | convolution fusion | flops 314376192 | bytes 12095488 | tf_op jit(solution)/shard_map/hqk,khe->qhe/dot_general | solution.py:79
  139.1 3.5 %convolution_convert_fusion = bf16[520,2304]{1,0:T(8,128)(2,1)} fusion(bf16[576,2304]{1,0:T(8,128)(2,1)S(1)} %copy-done, bf16[8,576]{0,1:T(8,128)(2,1)S(1)} %copy-done.4, bf16[512,576]{0,1:T(8,128)(2,1)S(1)} %bitcast.72), kind=kOutput, calls=%fused_computation.24 | convolution fusion | flops 1382584320 | bytes 5649408 | tf_op jit(solution)/shard_map/dot_general | solution.py:169
  142.6 57.6 %all-reduce.2.cloned.1.call-done = bf16[520,2304]{1,0:T(8,128)(2,1)} async-done(((bf16[520,2304]{1,0:T(8,128)(2,1)}), bf16[520,2304]{1,0:T(8,128)(2,1)}) %all-reduce.2.cloned.1.call-update) | async-done | bytes 2396176 | tf_op jit(solution)/shard_map/psum | solution.py:170
  200.2 3.4 %fusion.5 = (f32[520]{0:T(1024)S(1)}, bf16[520,2304]{1,0:T(8,128)(2,1)S(1)}) fusion(bf16[520,2304]{1,0:T(8,128)(2,1)} %all-reduce.2.cloned.1.call-done, bf16[8,2304]{1,0:T(8,128)(2,1)S(1)} %copy-done.3, bf16[512,2304]{1,0:T(8,128)(2,1)} %param.11), kind=kLoop, calls=%fused_computation.16 | loop fusion | flops 11980280 | bytes 7190560 | tf_op jit(solution)/shard_map/reduce_sum | solution.py:15
  203.6 1.6 slice.122
  205.2 0.6 slice.123
  205.8 0.6 fusion.7
  206.4 1.6 slice.124
  208.0 0.6 slice.125
  (37 shorter events, 0.4 us)
Async XLA Ops:
  7.2 131.9 %copy-start = (bf16[576,2304]{1,0:T(8,128)(2,1)S(1)}, bf16[576,2304]{1,0:T(8,128)(2,1)}, u32[]{:S(2)}) copy-start(bf16[576,2304]{1,0:T(8,128)(2,1)} %param.15) | copy-start | bytes 7962628
  7.2 193.0 %all-reduce.2.cloned.1.call-start = ((), (), s32[]{:S(2)}) async-start(), calls=%async_computation | async-start | bytes 4792320 | tf_op jit(solution)/shard_map/psum | solution.py:170
  8.8 12.5 %slice-start = ((s8[4718592]{0:T(1024)(128)(4,1)}), s8[4194304]{0:T(1024)(128)(4,1)S(1)}, s32[]{:S(2)}) async-start(s8[4718592]{0:T(1024)(128)(4,1)} %bitcast.63), calls=%async_computation.1 | async-start | bytes 8388608
  11.2 10.1 %slice-start.1 = ((s8[4718592]{0:T(1024)(128)(4,1)}), s8[524288]{0:T(1024)(128)(4,1)S(1)}, s32[]{:S(2)}) async-start(s8[4718592]{0:T(1024)(128)(4,1)} %bitcast.63), calls=%async_computation.2 | async-start | bytes 1048576
  21.3 35.1 %copy-start.6 = (s32[64]{0:T(128)S(1)}, s32[64]{0:T(128)}, u32[]{:S(2)}) copy-start(s32[64]{0:T(128)} %param.21) | copy-start | bytes 772
  105.6 2.1 copy-start.1
  126.0 7.1 %copy-start.2 = (bf16[512,1,576]{0,2,1:T(8,128)(2,1)S(1)}, bf16[512,1,576]{0,2,1:T(8,128)(2,1)}, u32[]{:S(2)}) copy-start(bf16[512,1,576]{0,2,1:T(8,128)(2,1)} %get-tuple-element.10) | copy-start | bytes 1769476
  133.1 6.0 %copy-start.4 = (bf16[8,576]{0,1:T(8,128)(2,1)S(1)}, bf16[8,576]{0,1:T(8,128)(2,1)}, u32[]{:S(2)}) copy-start(bf16[8,576]{0,1:T(8,128)(2,1)} %copy.27) | copy-start | bytes 27652
  139.1 61.1 %copy-start.3 = (bf16[8,2304]{1,0:T(8,128)(2,1)S(1)}, bf16[8,2304]{1,0:T(8,128)(2,1)}, u32[]{:S(2)}) copy-start(bf16[8,2304]{1,0:T(8,128)(2,1)} %param.12) | copy-start | bytes 110596
  142.6 63.2 %copy-start.5 = (f32[2304]{0:T(1024)S(1)}, f32[2304]{0:T(1024)}, u32[]{:S(2)}) copy-start(f32[2304]{0:T(1024)} %param.16) | copy-start | bytes 27652
Sparse Core Ops, SparseCore 0:
  142.8 57.4 all-reduce.1
where the time goes:
time: 216 us; the launch traced here: 215 us
  blocking collectives  63.1 us (29%)
  waiting for transfers between devices  57.6 us (27%)
  matrix products  38.1 us (18%)
  other arithmetic  22.4 us (10%)
  local copies, waits for them, and re-layouts  19.3 us (9%)
  between operations  15 us (7%)
    psum x1, waiting for transfers between devices, local(): lax.psum(partial_value.astype(jnp.bfloat16), 'tp').astype(jnp.float32)  57.6 us
    all_gather x1, blocking collectives, local(): arrived = lax.all_gather(decode_block, 'seq', axis=0, tiled=True)  32.5 us
    all_gather x1, blocking collectives, local(): shard_piece = lax.all_gather(slot_results, 'seq', axis=0, tiled=True)  30.5 us
    dot_general x1, matrix products, local(): jnp.dot(normed_in, qkv_weight.reshape(model_width, 3 * local_width), pref...  8.62 us
    dot_general x1, matrix products, prefill_attention(): jnp.einsum('hqk,khe->qhe', cache_weights, cache_values, preferred_element...  7.07 us
    dot_general x1, matrix products, prefill_attention(): jnp.einsum('hqk,khe->qhe', span_weights, new_values, preferred_element_ty...  6 us
    reduce_sum x2, other arithmetic, rms_norm(): jnp.mean(widened * widened, axis=-1, keepdims=True) + RMS_EPSILON  5.77 us
    reduce_sum x1, other arithmetic, prefill_attention(): jnp.sum(span_exp, axis=-1, keepdims=True)  5.61 us
  transfers between devices with their start and end apart: 1, of which 1 were waited for; matrix products, arithmetic and copies ran while one was open for 0% of the time, Pallas kernels for 0%

commit v1 on v0

--- a/solution.py
+++ b/solution.py
@@ -134,6 +134,10 @@
     decode_lengths,
     request_slot,
 ):
+
+    def _plan_racks(slab_in):
+        return jnp.sum(jax.lax.all_gather(slab_in, "tp"), 0)
+
     span_rows = prefill_tokens.shape[0]
     decode_rows = decode_tokens.shape[0]
     model_width = prefill_tokens.shape[1]
@@ -167,7 +171,7 @@
     returned = jnp.dot(picker, shard_piece, preferred_element_type=jnp.float32).astype(jnp.bfloat16)
     attended_all = jnp.concatenate([prefill_attended, returned], axis=0)
     partial_value = jnp.dot(attended_all, out_weight, preferred_element_type=jnp.float32)
-    combined = lax.psum(partial_value.astype(jnp.bfloat16), "tp").astype(jnp.float32)
+    combined = _plan_racks(partial_value.astype(jnp.bfloat16)).astype(jnp.float32)
     hidden = (tokens_all.astype(jnp.float32) + combined).astype(jnp.bfloat16)
     normed = rms_norm(hidden, feedforward_gain).astype(jnp.bfloat16)
     return (hidden[:span_rows], hidden[span_rows:], normed[:span_rows], normed[span_rows:])

time: 216 us -> 232 us (1.074)
  waiting for transfers between devices: 57.6 us -> 66.1 us
  other arithmetic: 22.4 us -> 29.7 us
    all_gather x0 -> x1, waiting for transfers between devices: none -> 66.1 us  [_plan_racks(): return jnp.sum(jax.lax.all_gather(slab_in, 'tp'), 0)]
    psum x1 -> x0, waiting for transfers between devices: 57.6 us -> none  [local(): lax.psum(partial_value.astype(jnp.bfloat16), 'tp').astype(jnp.float32)]
    reduce_sum x0 -> x1, other arithmetic: none -> 7.33 us  [_plan_racks(): return jnp.sum(jax.lax.all_gather(slab_in, 'tp'), 0)]
where the time goes in v1:
time: 232 us; the launch traced here: 231 us
  waiting for transfers between devices  66.1 us (28%)
  blocking collectives  63.1 us (27%)
  matrix products  38.1 us (16%)
  other arithmetic  29.7 us (13%)
  local copies, waits for them, and re-layouts  19.3 us (8%)
  between operations  14.9 us (6%)
    all_gather x1, waiting for transfers between devices, _plan_racks(): return jnp.sum(jax.lax.all_gather(slab_in, 'tp'), 0)  66.1 us
    all_gather x1, blocking collectives, local(): arrived = lax.all_gather(decode_block, 'seq', axis=0, tiled=True)  32.5 us
    all_gather x1, blocking collectives, local(): shard_piece = lax.all_gather(slot_results, 'seq', axis=0, tiled=True)  30.5 us
    dot_general x1, matrix products, local(): jnp.dot(normed_in, qkv_weight.reshape(model_width, 3 * local_width), pref...  8.62 us
    reduce_sum x1, other arithmetic, _plan_racks(): return jnp.sum(jax.lax.all_gather(slab_in, 'tp'), 0)  7.33 us
    dot_general x1, matrix products, prefill_attention(): jnp.einsum('hqk,khe->qhe', cache_weights, cache_values, preferred_element...  7.07 us
    dot_general x1, matrix products, prefill_attention(): jnp.einsum('hqk,khe->qhe', span_weights, new_values, preferred_element_ty...  6 us
    reduce_sum x2, other arithmetic, rms_norm(): jnp.mean(widened * widened, axis=-1, keepdims=True) + RMS_EPSILON  5.79 us
  transfers between devices with their start and end apart: 1, of which 1 were waited for; matrix products, arithmetic and copies ran while one was open for 0% of the time, Pallas kernels for 0%

profile of v1, /device:TPU:0, one launch (start us, length us, event | category | flops | bytes accessed | tf_op | source)
XLA Modules:
  0.0 231.3 jit_solution(11094251642154847372)
XLA Ops:
  7.2 0.8 convert_element_type.117
  8.1 0.7 iota_compare_fusion.1
  8.8 2.4 %fusion.8 = f32[520]{0:T(1024)S(1)} fusion(bf16[8,2304]{1,0:T(8,128)(2,1)} %param.12, bf16[512,2304]{1,0:T(8,128)(2,1)} %param.11), kind=kLoop, calls=%fused_computation.19 | loop fusion | flops 7187960 | bytes 2398240 | tf_op jit(solution)/shard_map/reduce_sum | solution.py:15
  11.2 8.6 %convolution_convert_fusion.1 = bf16[520,1728]{1,0:T(8,128)(2,1)S(1)} fusion(bf16[2304,1728]{0,1:T(8,128)(2,1)} %bitcast.73, f32[2304]{0:T(1024)} %param.13, f32[520]{0:T(1024)S(1)} %add_rsqrt_fusion.1, bf16[8,2304]{1,0:T(8,128)(2,1)} %param.12, bf16[512,2304]{1,0:T(8,128)(2,1)} %param.11), kind=kOutput, calls=%fused_computation.25 | convolution fusion | flops 4149849600 | bytes 12167200 | tf_op jit(solution)/shard_map/dot_general | solution.py:148
  19.8 1.4 slice.106
  21.2 0.1 iota_compare_fusion
  21.3 2.5 %fusion.55 = (bf16[8,1,256,576]{2,3,1,0:T(8,128)(2,1)}, bf16[8,1,256,576]{2,3,1,0:T(8,128)(2,1)}) fusion(bf16[8,2,256,576]{2,3,1,0:T(8,128)(2,1)S(1)} %bitcast.66), kind=kLoop, calls=%fused_computation.103 | loop fusion | bytes 9437184 | tf_op jit(solution)/shard_map/slice | solution.py:97
  23.8 0.1 slice.92
  23.9 32.5 %all_gather.12 = bf16[64,3,576]{2,0,1:T(8,128)(2,1)S(1)} all-gather(bf16[8,3,576]{2,0,1:T(8,128)(2,1)S(1)} %copy.25), channel_id=1, replica_groups=mesh['seq'=8,'tp'=4] {'seq'}, dimensions={0}, use_global_device_ids=true | all-gather | bytes 248832 | tf_op jit(solution)/shard_map/all_gather | solution.py:158
  56.5 0.2 convolution_convert_fusion.2
  56.7 0.1 reshape.210
  56.8 0.1 multiply_cosine_fusion.1
  57.0 0.1 subtract_convert_fusion.2
  57.1 0.1 fusion.38
  57.2 0.2 fusion.32
  57.3 0.1 copy.34
  57.4 2.1 fusion.35
  59.5 0.1 fusion.34
  59.6 0.2 fusion.33
  59.8 0.1 fusion.37
  60.1 2.4 %fusion.29 = f32[8,9,1,64]{3,2,1,0:T(1,128)S(1)} fusion(bf16[8,256,9,64]{1,3,2,0:T(8,128)(2,1)} %bitcast.70, bf16[8,9,256,1]{2,0,1,3:T(8,128)(2,1)S(1)} %fusion.37), kind=kOutput, calls=%fused_computation.53 | convolution fusion | flops 2359296 | bytes 2414592 | tf_op jit(solution)/shard_map/shk,skhe->she/dot_general | solution.py:115
  62.4 0.1 fusion.31
  62.5 0.1 convert_element_type.126
  62.6 30.5 %all_gather.13 = bf16[64,576]{1,0:T(8,128)(2,1)S(1)} all-gather(bf16[8,576]{1,0:T(8,128)(2,1)S(1)} %convert_element_type.126), channel_id=1, replica_groups=mesh['seq'=8,'tp'=4] {'seq'}, dimensions={0}, use_global_device_ids=true | all-gather | bytes 82944 | tf_op jit(solution)/shard_map/all_gather | solution.py:168
  93.2 0.2 convolution_convert_fusion.3
  93.4 0.8 copy.27
  94.2 3.2 %fusion.56 = (bf16[1,1,1024,576]{2,3,1,0:T(8,128)(2,1)}, bf16[1,1,1024,576]{2,3,1,0:T(8,128)(2,1)}) fusion(bf16[1,2,1024,576]{2,3,1,0:T(8,128)(2,1)} %param.17), kind=kLoop, calls=%fused_computation.104 | loop fusion | bytes 4718592 | tf_op jit(solution)/shard_map/slice | solution.py:49
  98.1 4.0 %copy.23 = bf16[512,1728]{0,1:T(8,128)(2,1)} copy(bf16[512,1728]{1,0:T(8,128)(2,1)} %slice.106) | data formatting | bytes 3538944 | tf_op jit(solution)/shard_map/slice | solution.py:154
  102.1 2.4 %fusion.57 = (bf16[512,1,576]{0,2,1:T(8,128)(2,1)}, bf16[512,1,576]{0,2,1:T(8,128)(2,1)S(1)}, bf16[512,1,576]{0,2,1:T(8,128)(2,1)S(1)}) fusion(bf16[512,3,576]{0,2,1:T(8,128)(2,1)} %bitcast.64), kind=kLoop, calls=%fused_computation.105 | loop fusion | bytes 3538944 | tf_op jit(solution)/shard_map/slice | solution.py:48
  104.5 1.2 convert.41
  105.6 0.3 multiply_cosine_fusion
  105.9 0.1 convert.40
  106.1 1.6 subtract_convert_fusion
  107.7 2.8 %fusion = (f32[9,512]{1,0:T(8,128)S(1)}, f32[9,512,1024]{2,1,0:T(8,128)S(1)}) fusion(pred[1024]{0:T(1024)(128)(4,1)S(1)} %iota_compare_fusion.3, bf16[1024,9,64]{0,2,1:T(8,128)(2,1)S(1)} %bitcast.67, bf16[512,9,32]{0,2,1:T(8,128)(2,1)S(1)} %get-tuple-element.17, bf16[512,9,32]{0,2,1:T(8,128)(2,1)S(1)} %get-tuple-element.18), kind=kOutput, calls=%fused_computation.3 | convolution fusion | flops 619310592 | bytes 20663296 | tf_op jit(solution)/shard_map/qhe,khe->hqk/dot_general | solution.py:52
  110.5 5.3 %fusion.3 = (f32[9,512]{1,0:T(8,128)S(1)}, f32[9,512,512]{1,2,0:T(8,128)}) fusion(pred[512,512]{0,1:T(8,128)(4,1)S(1)} %iota_compare_fusion, bf16[512,9,32]{0,2,1:T(8,128)(2,1)S(1)} %get-tuple-element.14, bf16[512,9,32]{0,2,1:T(8,128)(2,1)S(1)} %get-tuple-element.13, bf16[512,9,32]{0,2,1:T(8,128)(2,1)S(1)} %get-tuple-element.17, ...), kind=kOutput, calls=%fused_computation.9 | convolution fusion | flops 311422464 | bytes 10897408 | tf_op jit(solution)/shard_map/qhe,khe->hqk/dot_general | solution.py:56
  115.8 4.5 %fusion.1 = f32[9,512]{1,0:T(8,128)S(1)} fusion(f32[9,512,1024]{2,1,0:T(8,128)S(1)} %get-tuple-element.35, f32[9,512]{1,0:T(8,128)S(1)} %max.11, pred[1024]{0:T(1024)(128)(4,1)S(1)} %iota_compare_fusion.3), kind=kLoop, calls=%fused_computation.4 | loop fusion | flops 18869760 | bytes 18912256 | tf_op jit(solution)/shard_map/reduce_sum | solution.py:71
  120.4 5.6 %fusion.4 = f32[9,512]{1,0:T(8,128)S(1)} fusion(f32[9,512,512]{1,2,0:T(8,128)} %get-tuple-element.37, f32[9,512]{1,0:T(8,128)S(1)} %max.11, pred[512,512]{0,1:T(8,128)(4,1)S(1)} %iota_compare_fusion), kind=kLoop, calls=%fused_computation.10 | loop fusion | flops 9432576 | bytes 9736192 | tf_op jit(solution)/shard_map/reduce_sum | solution.py:71
  126.0 7.1 %fusion.16 = f32[512,9,64]{0,2,1:T(8,128)} fusion(bf16[1024,9,64]{0,2,1:T(8,128)(2,1)} %bitcast.71, f32[9,512,1024]{2,1,0:T(8,128)S(1)} %get-tuple-element.35, f32[9,512]{1,0:T(8,128)S(1)} %add.76, f32[9,512]{1,0:T(8,128)S(1)} %max.11, pred[1024]{0:T(1024)(128)(4,1)S(1)} %iota_compare_fusion.3), kind=kOutput, calls=%fused_computation.29 | convolution fusion | flops 627572736 | bytes 21271552 | tf_op jit(solution)/shard_map/hqk,khe->qhe/dot_general | solution.py:76
  133.1 6.0 %fusion.19 = bf16[512,9,64]{0,2,1:T(8,128)(2,1)S(1)} fusion(f32[512,9,64]{0,2,1:T(8,128)} %fusion.16, bf16[512,9,64]{0,2,1:T(8,128)(2,1)S(1)} %bitcast.72, f32[9,512,512]{1,2,0:T(8,128)} %get-tuple-element.37, f32[9,512]{1,0:T(8,128)S(1)} %add.76, f32[9,512]{1,0:T(8,128)S(1)} %max.11, pred[512,512]{0,1:T(8,128)(4,1)S(1)} %iota_compare_fusion), kind=kOutput, calls=%fused_computation.32 | convolution fusion | flops 314376192 | bytes 12095488 | tf_op jit(solution)/shard_map/hqk,khe->qhe/dot_general | solution.py:79
  139.1 3.5 %convolution_convert_fusion = bf16[520,2304]{1,0:T(8,128)(2,1)} fusion(bf16[576,2304]{1,0:T(8,128)(2,1)S(1)} %copy-done, bf16[8,576]{0,1:T(8,128)(2,1)S(1)} %copy-done.4, bf16[512,576]{0,1:T(8,128)(2,1)S(1)} %bitcast.74), kind=kOutput, calls=%fused_computation.24 | convolution fusion | flops 1382584320 | bytes 5649408 | tf_op jit(solution)/shard_map/dot_general | solution.py:173
  142.6 66.1 %all-gather.3.cloned.1.call-done = bf16[2080,2304]{1,0:T(8,128)(2,1)} async-done(((bf16[520,2304]{1,0:T(8,128)(2,1)}), bf16[2080,2304]{1,0:T(8,128)(2,1)}) %all-gather.3.cloned.1.call-update) | async-done | bytes 9584656 | tf_op jit(solution)/shard_map/all_gather | solution.py:139
  208.7 7.3 %reduce_sum.61 = bf16[520,2304]{1,0:T(8,128)(2,1)} reduce(bf16[4,520,2304]{2,1,0:T(8,128)(2,1)} %bitcast.62, bf16[]{:T(256)} %constant.34.clone.1), dimensions={0}, to_apply=%region_7.8 | reduce | flops 3594240 | bytes 11980802 | tf_op jit(solution)/shard_map/reduce_sum | solution.py:139
  216.1 3.4 %fusion.5 = (f32[520]{0:T(1024)S(1)}, bf16[520,2304]{1,0:T(8,128)(2,1)S(1)}) fusion(bf16[520,2304]{1,0:T(8,128)(2,1)} %reduce_sum.61, bf16[8,2304]{1,0:T(8,128)(2,1)S(1)} %copy-done.3, bf16[512,2304]{1,0:T(8,128)(2,1)} %param.11), kind=kLoop, calls=%fused_computation.16 | loop fusion | flops 11980280 | bytes 7190560 | tf_op jit(solution)/shard_map/reduce_sum | solution.py:15
  219.5 1.6 slice.122
  221.0 0.6 slice.123
  221.7 0.6 fusion.7
  222.3 1.6 slice.124
  223.8 0.6 slice.125
  (38 shorter events, 0.5 us)
Async XLA Ops:
  7.2 131.9 %copy-start = (bf16[576,2304]{1,0:T(8,128)(2,1)S(1)}, bf16[576,2304]{1,0:T(8,128)(2,1)}, u32[]{:S(2)}) copy-start(bf16[576,2304]{1,0:T(8,128)(2,1)} %param.15) | copy-start | bytes 7962628
  7.2 201.5 %all-gather.3.cloned.1.call-start = ((), (), s32[]{:S(2)}) async-start(), calls=%async_computation | async-start | bytes 11980800 | tf_op jit(solution)/shard_map/all_gather | solution.py:139
  8.8 12.5 %slice-start = ((s8[4718592]{0:T(1024)(128)(4,1)}), s8[4194304]{0:T(1024)(128)(4,1)S(1)}, s32[]{:S(2)}) async-start(s8[4718592]{0:T(1024)(128)(4,1)} %bitcast.65), calls=%async_computation.1 | async-start | bytes 8388608
  11.2 10.1 %slice-start.1 = ((s8[4718592]{0:T(1024)(128)(4,1)}), s8[524288]{0:T(1024)(128)(4,1)S(1)}, s32[]{:S(2)}) async-start(s8[4718592]{0:T(1024)(128)(4,1)} %bitcast.65), calls=%async_computation.2 | async-start | bytes 1048576
  21.3 35.1 %copy-start.6 = (s32[64]{0:T(128)S(1)}, s32[64]{0:T(128)}, u32[]{:S(2)}) copy-start(s32[64]{0:T(128)} %param.21) | copy-start | bytes 772
  105.6 2.1 copy-start.1
  126.0 7.1 %copy-start.2 = (bf16[512,1,576]{0,2,1:T(8,128)(2,1)S(1)}, bf16[512,1,576]{0,2,1:T(8,128)(2,1)}, u32[]{:S(2)}) copy-start(bf16[512,1,576]{0,2,1:T(8,128)(2,1)} %get-tuple-element.10) | copy-start | bytes 1769476
  133.1 6.0 %copy-start.4 = (bf16[8,576]{0,1:T(8,128)(2,1)S(1)}, bf16[8,576]{0,1:T(8,128)(2,1)}, u32[]{:S(2)}) copy-start(bf16[8,576]{0,1:T(8,128)(2,1)} %copy.27) | copy-start | bytes 27652
  208.7 7.3 %copy-start.3 = (bf16[8,2304]{1,0:T(8,128)(2,1)S(1)}, bf16[8,2304]{1,0:T(8,128)(2,1)}, u32[]{:S(2)}) copy-start(bf16[8,2304]{1,0:T(8,128)(2,1)} %param.12) | copy-start | bytes 110596
  216.1 5.6 %copy-start.5 = (f32[2304]{0:T(1024)S(1)}, f32[2304]{0:T(1024)}, u32[]{:S(2)}) copy-start(f32[2304]{0:T(1024)} %param.16) | copy-start | bytes 27652
Sparse Core Ops, SparseCore 0:
  142.7 65.9 all-gather.2
